TPU v7x, 32 devices: a whole 2x2x4 slice. The times are simulated.
32 devices in a mesh: dp: 2 (over x), ha: 4 (over z), wa: 4 (over y, core).
Axes of the slice: x: 2, y: 2, z: 4, core: 2. Of those that a mesh axis runs over, the one named last changes fastest.
Arguments:
- query_in: bfloat16 [2, 4, 4, 384, 512], P('dp', 'ha', 'wa'), may hold values from -30 to 30
- key_in: bfloat16 [2, 4, 4, 384, 512], P('dp', 'ha', 'wa'), may hold values from -6 to 6
- value_in: bfloat16 [2, 4, 4, 384, 512], P('dp', 'ha', 'wa'), may hold values from -6 to 6
- grad_out: bfloat16 [2, 4, 4, 384, 3072], P('dp', 'ha', 'wa'), may hold values from -1.5 to 1.5
- out_weight: bfloat16 [512, 3072], P('dp'), may hold values from -0.25 to 0.25
Outputs:
- outcome: bfloat16 [2, 4, 4, 384, 3072], P('dp', 'ha', 'wa')
- query_grad: float32 [2, 4, 4, 384, 512], P('dp', 'ha', 'wa')
- key_grad: float32 [2, 4, 4, 384, 512], P('dp', 'ha', 'wa')
- value_grad: float32 [2, 4, 4, 384, 512], P('dp', 'ha', 'wa')
- weight_grad: float32 [512, 3072], P('dp')
All inputs are finite; a program needn't handle non-finite values.
Results may differ from a plain program's by a relative error of at most 0.035.
Values may be sent and summed in bfloat16 or wider, within the bound.
No kernel may reach another device: no remote copies, remote signals or barrier semaphores. Data moves between devices by JAX's collectives and lax.ppermute only.
A program may use at most 192 MiB of HBM per device.

v0:
```python
import jax
import jax.numpy as jnp
from jax import lax
from jax.sharding import PartitionSpec as P

HEADS = 4
SCALE_POWER = -0.5


def shortened(array):
    return jax.tree.map(lambda a: a.astype(jnp.bfloat16) if a.dtype == jnp.float32 else a, array)


def shifted(value, axis, steps):
    count = lax.axis_size(axis)
    first, last = (max(0, -steps), min(count, count - steps))
    return lax.ppermute(value, axis, [(source, source + steps) for source in range(first, last)])


def with_halo(array, sides, width):
    for axis, dim in sides:
        peers, length = (lax.axis_size(axis), array.shape[dim])
        up = [(i, (i + 1) % peers) for i in range(peers - 1)]
        down = [(j, i) for i, j in up]
        last = lax.slice_in_dim(array, length - width, length, axis=dim)
        first = lax.slice_in_dim(array, 0, width, axis=dim)
        before = lax.ppermute(last, axis, up)
        after = lax.ppermute(first, axis, down)
        array = jnp.concatenate([before, array, after], axis=dim)
    return array


def product(pattern, first_op, second_op):
    return jnp.einsum(pattern, first_op, second_op, preferred_element_type=jnp.float32)


def stack_window(extended, tile_cols):
    window_parts = []
    for row_off in range(3):
        for col_off in range(3):
            window_parts.append(extended[row_off, col_off : col_off + tile_cols])
    stacked = jnp.stack(window_parts, axis=1)
    return stacked.reshape((tile_cols, 9 * stacked.shape[2]) + stacked.shape[3:])


def window_keep(row_ok, col_ok, tile_cols, tile_len):
    flag_list = []
    for row_off in range(3):
        for col_off in range(3):
            flag_list.append(
                jnp.logical_and(row_ok[row_off], col_ok[col_off : col_off + tile_cols])
            )
    stacked = jnp.stack(flag_list, axis=1)
    return jnp.repeat(stacked, tile_len, axis=1)


def spread_window(stacked, tile_cols, tile_len):
    window_parts = stacked.reshape((tile_cols, 3, 3, tile_len) + stacked.shape[2:])
    spread_rows = []
    for row_off in range(3):
        gathered = None
        for col_off in range(3):
            placed = jnp.pad(
                window_parts[:, row_off, col_off], ((col_off, 2 - col_off), (0, 0), (0, 0))
            )
            gathered = placed if gathered is None else gathered + placed
        spread_rows.append(gathered)
    return jnp.stack(spread_rows)


def widen_rim(edge_part, axis_pos, length, at_first):
    expanded = jnp.expand_dims(edge_part, axis_pos)
    pad_spec = [(0, 0)] * expanded.ndim
    pad_spec[axis_pos] = (0, length - 1) if at_first else (length - 1, 0)
    return jnp.pad(expanded, pad_spec)


def attend_row(query_row, key_ext, value_ext, visible, head_count):
    tile_cols, tile_len, feature_width = query_row.shape
    head_dim = feature_width // head_count
    score_scale = head_dim**SCALE_POWER
    query_heads = query_row.reshape(tile_cols, tile_len, head_count, head_dim)
    key_heads = stack_window(key_ext, tile_cols).reshape(
        tile_cols, 9 * tile_len, head_count, head_dim
    )
    value_heads = stack_window(value_ext, tile_cols).reshape(
        tile_cols, 9 * tile_len, head_count, head_dim
    )
    scores = product("jqhd,jkhd->jhqk", query_heads, key_heads) * score_scale
    scores = jnp.where(visible[:, None, None, :], scores, -1e30)
    row_max = jnp.max(scores, axis=-1, keepdims=True)
    log_norm = row_max + jnp.log(jnp.sum(jnp.exp(scores - row_max), axis=-1, keepdims=True))
    soft_probs = jnp.exp(scores - log_norm).astype(jnp.bfloat16)
    attended = product("jhqk,jkhd->jqhd", soft_probs, value_heads)
    attended = attended.reshape(tile_cols, tile_len, feature_width).astype(jnp.bfloat16)
    return (attended, soft_probs, log_norm[..., 0])


def query_back(query_row, key_ext, value_ext, attended, grad_attn, soft_probs, head_count):
    tile_cols, tile_len, feature_width = query_row.shape
    head_dim = feature_width // head_count
    score_scale = head_dim**SCALE_POWER
    attended_heads = attended.astype(jnp.float32).reshape(tile_cols, tile_len, head_count, head_dim)
    grad_heads = grad_attn.reshape(tile_cols, tile_len, head_count, head_dim)
    row_delta = jnp.sum(attended_heads * grad_heads.astype(jnp.float32), axis=-1)
    row_delta = jnp.transpose(row_delta, (0, 2, 1))
    value_heads = stack_window(value_ext, tile_cols).reshape(
        tile_cols, 9 * tile_len, head_count, head_dim
    )
    prob_grad = product("jqhd,jkhd->jhqk", grad_heads, value_heads)
    score_grad = (soft_probs.astype(jnp.float32) * (prob_grad - row_delta[..., None])).astype(
        jnp.bfloat16
    )
    key_heads = stack_window(key_ext, tile_cols).reshape(
        tile_cols, 9 * tile_len, head_count, head_dim
    )
    query_grad = product("jhqk,jkhd->jqhd", score_grad, key_heads) * score_scale
    query_grad = query_grad.reshape(tile_cols, tile_len, feature_width)
    query_heads = query_row.reshape(tile_cols, tile_len, head_count, head_dim)
    key_part = (product("jhqk,jqhd->jkhd", score_grad, query_heads) * score_scale).reshape(
        tile_cols, 9 * tile_len, feature_width
    )
    value_part = product("jhqk,jqhd->jkhd", soft_probs, grad_heads).reshape(
        tile_cols, 9 * tile_len, feature_width
    )
    return (
        query_grad,
        row_delta,
        spread_window(key_part, tile_cols, tile_len),
        spread_window(value_part, tile_cols, tile_len),
    )


def send_rows(edge_part, offset):
    return shifted(shortened(edge_part), "ha", offset).astype(edge_part.dtype)


def send_columns(edge_part, offset):
    return shifted(shortened(edge_part), "wa", offset).astype(edge_part.dtype)


def on_device(query_in, key_in, value_in, grad_out, out_weight):
    clip_count, tile_rows, tile_cols, tile_len, feature_width = query_in.shape
    model_width = grad_out.shape[-1]
    head_count = HEADS
    row_first = lax.axis_index("ha") * tile_rows
    col_first = lax.axis_index("wa") * tile_cols
    all_rows = tile_rows * lax.axis_size("ha")
    all_cols = tile_cols * lax.axis_size("wa")
    row_global = row_first - 1 + jnp.arange(tile_rows + 2, dtype=jnp.int32)
    row_flags = jnp.logical_and(row_global >= 0, row_global < all_rows)
    col_global = col_first - 1 + jnp.arange(tile_cols + 2, dtype=jnp.int32)
    col_ok = jnp.logical_and(col_global >= 0, col_global < all_cols)
    full_weight = lax.all_gather(out_weight, "dp", axis=0, tiled=True)
    flat_grad = grad_out.reshape(-1, model_width)
    grad_attn = lax.dot_general(
        flat_grad, full_weight, (((1,), (1,)), ((), ())), preferred_element_type=jnp.float32
    )
    grad_attn = grad_attn.astype(jnp.bfloat16).reshape(query_in.shape)
    extended = with_halo(jnp.stack([key_in, value_in]), (("ha", 2), ("wa", 3)), 1)
    key_ext_all = extended[0]
    value_ext_all = extended[1]
    row_total = clip_count * tile_rows
    flat_rows = jnp.arange(row_total, dtype=jnp.int32)
    query_rows = query_in.reshape(row_total, tile_cols, tile_len, feature_width)
    grad_rows = grad_attn.reshape(row_total, tile_cols, tile_len, feature_width)

    def row_window(extended_all):
        return extended_all[0]

    def row_keep():
        return window_keep(row_flags, col_ok, tile_cols, tile_len)

    def forward_row(inputs):
        query_row, flat_index = inputs
        return attend_row(
            query_row, row_window(key_ext_all), row_window(value_ext_all), row_keep(), head_count
        )

    attended, soft_probs, log_norm = lax.map(forward_row, (query_rows, flat_rows))
    flat_attn = attended.reshape(-1, feature_width)
    outcome = jnp.dot(flat_attn, full_weight, preferred_element_type=jnp.float32).astype(
        jnp.bfloat16
    )
    outcome = outcome.reshape(clip_count, tile_rows, tile_cols, tile_len, model_width)

    def query_side(inputs):
        query_row, grad_row, attended_row, probs_row, flat_index = inputs
        query_grad, row_delta, key_part, value_part = query_back(
            query_row,
            row_window(key_ext_all),
            row_window(value_ext_all),
            attended_row,
            grad_row,
            probs_row,
            head_count,
        )
        return (query_grad, jnp.stack([key_part, value_part]))

    query_grad, ext_parts = lax.map(
        query_side, (query_rows, grad_rows, attended, soft_probs, flat_rows)
    )
    ext_parts = ext_parts.reshape(
        clip_count, tile_rows, 2, 3, tile_cols + 2, tile_len, feature_width
    )
    padded_grad = None
    for row_off in range(3):
        placed = jnp.pad(
            ext_parts[:, :, :, row_off],
            ((0, 0), (row_off, 2 - row_off), (0, 0), (0, 0), (0, 0), (0, 0)),
        )
        padded_grad = placed if padded_grad is None else padded_grad + placed
    from_below = send_rows(padded_grad[:, 0], -1)
    from_above = send_rows(padded_grad[:, tile_rows + 1], 1)
    middle = padded_grad[:, 1 : tile_rows + 1]
    middle = (
        middle
        + widen_rim(from_below, 1, tile_rows, False)
        + widen_rim(from_above, 1, tile_rows, True)
    )
    from_right = send_columns(middle[:, :, :, 0], -1)
    from_left = send_columns(middle[:, :, :, tile_cols + 1], 1)
    core_part = middle[:, :, :, 1 : tile_cols + 1]
    core_part = (
        core_part
        + widen_rim(from_right, 3, tile_cols, False)
        + widen_rim(from_left, 3, tile_cols, True)
    )
    key_grad = core_part[:, :, 0]
    value_grad = core_part[:, :, 1]
    query_grad = query_grad.reshape(query_in.shape)
    row_share = feature_width // lax.axis_size("dp")
    local_term = lax.dot_general(
        flat_attn, flat_grad, (((0,), (0,)), ((), ())), preferred_element_type=jnp.float32
    )
    summed = lax.psum(local_term, ("dp", "ha", "wa"))
    weight_grad = lax.dynamic_slice_in_dim(summed, lax.axis_index("dp") * row_share, row_share, 0)
    return (outcome, query_grad, key_grad, value_grad, weight_grad)


def solution(mesh):
    return jax.shard_map(
        on_device,
        mesh=mesh,
        in_specs=(
            P("dp", "ha", "wa", None, None),
            P("dp", "ha", "wa", None, None),
            P("dp", "ha", "wa", None, None),
            P("dp", "ha", "wa", None, None),
            P("dp", None),
        ),
        out_specs=(
            P("dp", "ha", "wa", None, None),
            P("dp", "ha", "wa", None, None),
            P("dp", "ha", "wa", None, None),
            P("dp", "ha", "wa", None, None),
            P("dp", None),
        ),
        check_vma=False,
    )
```

profile of v0, /device:TPU:0, one launch (start us, length us, event | category | flops | bytes accessed | tf_op | source)
XLA Modules:
  0.0 480.3 jit_solution(6171080770053422806)
XLA Ops:
  10.5 5.6 %collective-permute-start = (bf16[2,1,1,1,384,512]{5,4,3,2,1,0:T(8,128)(2,1)S(1)}, bf16[2,1,1,1,384,512]{5,4,3,2,1,0:T(8,128)(2,1)S(1)}, u32[]{:S(2)}, u32[]{:S(2)}) collective-permute-start(bf16[2,1,1,1,384,512]{5,4,3,2,1,0:T(8,128)(2,1)S(1)} %pad_maximum_fusion.4), channel_id=1, source_target_pairs={{0,4},{4,8},{8,12},{1,5},{5,9},{9,13},{2,6},{6,10},{10,14},{3,7},{... | collective-permute-start | bytes 2359304 | tf_op jit(solution)/shard_map/ppermute | solution.py:27
  16.1 15.6 %collective-permute-done.1 = bf16[2,1,1,1,384,512]{5,4,3,2,1,0:T(8,128)(2,1)S(1)} collective-permute-done((bf16[2,1,1,1,384,512]{5,4,3,2,1,0:T(8,128)(2,1)S(1)}, bf16[2,1,1,1,384,512]{5,4,3,2,1,0:T(8,128)(2,1)S(1)}, u32[]{:S(2)}, u32[]{:S(2)}) %collective-permute-start.1) | collective-permute-done | bytes 786464 | tf_op jit(solution)/shard_map/ppermute | solution.py:28
  37.2 4.5 collective-permute-start.2
  71.5 7.2 %reshape.242 = bf16[3456,4,128]{2,1,0:T(4,128)(2,1)} reshape(bf16[1,9,384,512]{3,2,1,0:T(8,128)(2,1)} %pad_maximum_fusion.2) | data formatting | bytes 7077888 | tf_op jit(solution)/shard_map/reshape.31
  78.7 6.9 %copy.102 = bf16[3456,4,128]{0,2,1:T(8,128)(2,1)} copy(bf16[3456,4,128]{2,1,0:T(4,128)(2,1)} %reshape.242) | data formatting | bytes 7077888 | tf_op jit(solution)/shard_map/reshape.31
  85.6 7.5 %bitcast_reduce_fusion = (f32[4,384]{1,0:T(4,128)S(1)}, f32[4,3456,384]{2,1,0:T(8,128)S(1)}) fusion(pred[3456]{0:T(1024)(128)(4,1)S(1)} %broadcast_in_dim.69, bf16[3456,4,128]{0,2,1:T(8,128)(2,1)} %copy.102, bf16[384,4,128]{2,1,0:T(4,128)(2,1)S(1)} %copy-done.9), kind=kOutput, calls=%fused_computation.2 | convolution fusion | flops 1374878208 | bytes 25175424 | tf_op jit(solution)/shard_map/while/body/eval_jaxpr/jqhd,jkhd->jhqk/dot_general | solution.py:34
  93.1 5.7 %fusion.1 = f32[4,384]{1,0:T(4,128)S(1)} fusion(f32[4,3456,384]{2,1,0:T(8,128)S(1)} %get-tuple-element.125, f32[4,384]{1,0:T(4,128)S(1)} %get-tuple-element.124, pred[3456]{0:T(1024)(128)(4,1)S(1)} %broadcast_in_dim.69), kind=kLoop, calls=%fused_computation.4 | loop fusion | flops 21232128 | bytes 21249408 | tf_op jit(solution)/shard_map/while/body/eval_jaxpr/reduce_sum | solution.py:92
  98.8 7.5 %fusion.3 = bf16[4,384,3456]{1,2,0:T(8,128)(2,1)} fusion(f32[4,3456,384]{2,1,0:T(8,128)S(1)} %get-tuple-element.125, f32[4,384]{1,0:T(4,128)S(1)} %log_add_fusion, pred[3456]{0:T(1024)(128)(4,1)S(1)} %broadcast_in_dim.69), kind=kLoop, calls=%fused_computation.6 | loop fusion | flops 21233664 | bytes 31860096 | tf_op jit(solution)/shard_map/while/body/eval_jaxpr/convert_element_type | solution.py:93
  108.2 7.4 %reshape.241 = bf16[3456,4,128]{2,1,0:T(4,128)(2,1)} reshape(bf16[1,9,384,512]{3,2,1,0:T(8,128)(2,1)} %pad_maximum_fusion.1) | data formatting | bytes 7077888 | tf_op jit(solution)/shard_map/reshape.41
  115.6 10.2 %convolution_bitcast_fusion = f32[1,3456,4,128]{1,3,2,0:T(8,128)} fusion(bf16[384,4,128]{0,2,1:T(8,128)(2,1)S(1)} %bitcast.185, bf16[4,384,3456]{1,2,0:T(8,128)(2,1)} %fusion.3), kind=kOutput, calls=%fused_computation.15 | convolution fusion | flops 1358954496 | bytes 18087936 | tf_op jit(solution)/shard_map/while/body/eval_jaxpr/jhqk,jqhd->jkhd/dot_general | solution.py:34
  125.8 6.3 %multiply_reduce_fusion = (f32[384,4]{0,1:T(4,128)S(1)}, bf16[4,128,384]{2,1,0:T(8,128)(2,1)S(1)}) fusion(f32[1,384,4,128]{1,3,2,0:T(8,128)S(1)} %bitcast.195, bf16[4,384,3456]{1,2,0:T(8,128)(2,1)} %fusion.3, bf16[3456,4,128]{2,1,0:T(4,128)(2,1)S(1)} %copy-done.2), kind=kOutput, calls=%fused_computation.75 | convolution fusion | flops 1359739392 | bytes 15341568 | tf_op jit(solution)/shard_map/while/body/eval_jaxpr/jhqk,jkhd->jqhd/dot_general | solution.py:34
  132.1 12.1 %multiply_convert_fusion = bf16[4,384,3456]{1,2,0:T(8,128)(2,1)} fusion(bf16[4,384,3456]{1,2,0:T(8,128)(2,1)} %fusion.3, bf16[384,4,128]{0,2,1:T(8,128)(2,1)S(1)} %bitcast.186, f32[4,384]{1,0:T(4,128)S(1)} %bitcast.197, bf16[3456,4,128]{2,1,0:T(4,128)(2,1)} %reshape.241), kind=kOutput, calls=%fused_computation.7 | convolution fusion | flops 1380188160 | bytes 25171968 | tf_op jit(solution)/shard_map/while/body/eval_jaxpr/jqhd,jkhd->jhqk/dot_general | solution.py:34
  144.2 9.2 %copy.108 = f32[1,3456,4,128]{3,2,0,1:T(4,128)} copy(f32[1,3456,4,128]{1,3,2,0:T(8,128)} %convolution_bitcast_fusion) | data formatting | bytes 14155776 | tf_op jit(solution)/shard_map/while/body/eval_jaxpr/jhqk,jqhd->jkhd/transpose | solution.py:34
  153.4 8.4 %slice_bitcast_fusion.23 = (f32[1,384,512]{2,0,1:T(1,128)S(1)}, f32[1,384,512]{2,0,1:T(1,128)}, f32[1,384,512]{2,0,1:T(1,128)}, f32[1,384,512]{2,0,1:T(1,128)}, ...) fusion(f32[1,3,3,384,512]{4,0,3,2,1:T(1,128)} %bitcast.183), kind=kLoop, calls=%fused_computation.64 | loop fusion | bytes 14155776 | tf_op jit(solution)/shard_map/while/body/eval_jaxpr/squeeze | solution.py:64
  164.7 15.1 %copy.105 = f32[1,3456,4,128]{3,2,0,1:T(4,128)S(1)} copy(f32[1,3456,4,128]{3,1,2,0:T(8,128)S(1)} %multiply_bitcast_fusion) | data formatting | bytes 14155776 | tf_op jit(solution)/shard_map/while/body/eval_jaxpr/mul | solution.py:120
  179.8 4.1 slice_bitcast_fusion.32
  193.5 9.7 %maximum_bitcast_fusion.2 = f32[1,3,3,384,512]{4,2,3,1,0:T(4,128)} fusion(f32[1,3,384,512]{3,1,2,0:T(4,128)} %add_bitcast_fusion, f32[1,3,384,512]{3,1,2,0:T(4,128)} %add_bitcast_fusion.1, f32[1,3,384,512]{3,1,2,0:T(4,128)} %add_bitcast_fusion.2), kind=kLoop, calls=%fused_computation.12 | loop fusion | flops 3538944 | bytes 14155776 | tf_op jit(solution)/shard_map/while/body/eval_jaxpr/stack | solution.py:198
  203.2 4.5 add_bitcast_fusion.3
  214.5 9.7 %maximum_bitcast_fusion.1 = f32[1,3,3,384,512]{4,2,3,1,0:T(4,128)} fusion(f32[1,3,384,512]{3,1,2,0:T(4,128)} %add_bitcast_fusion.3, f32[1,3,384,512]{3,1,2,0:T(4,128)} %add_bitcast_fusion.4, f32[1,3,384,512]{3,1,2,0:T(4,128)} %add_bitcast_fusion.5), kind=kLoop, calls=%fused_computation.11 | loop fusion | flops 3538944 | bytes 14155776 | tf_op jit(solution)/shard_map/while/body/eval_jaxpr/stack | solution.py:198
  224.2 10.5 %maximum_bitcast_fusion = f32[1,1,2,3,3,384,512]{6,4,5,3,2,1,0:T(4,128)S(1)} fusion(f32[1,3,3,384,512]{4,2,3,1,0:T(4,128)} %maximum_bitcast_fusion.2, f32[1,3,3,384,512]{4,2,3,1,0:T(4,128)} %maximum_bitcast_fusion.1), kind=kLoop, calls=%fused_computation.9 | loop fusion | flops 3538944 | bytes 28311552 | tf_op jit(solution)/shard_map/reshape | solution.py:203
  234.6 7.7 %slice_bitcast_fusion.2 = (f32[1,1,2,3,384,512]{5,3,4,2,1,0:T(4,128)}, f32[1,1,2,3,384,512]{5,3,4,2,1,0:T(4,128)}, f32[1,1,2,3,384,512]{5,3,4,2,1,0:T(4,128)}) fusion(f32[1,1,2,3,3,384,512]{6,4,5,3,2,1,0:T(4,128)S(1)} %maximum_bitcast_fusion), kind=kLoop, calls=%fused_computation.20 | loop fusion | bytes 28311552 | tf_op jit(solution)/shard_map/squeeze | solution.py:209
  242.3 18.2 %pad_add_fusion = (f32[1,3,2,3,384,512]{5,3,4,2,1,0:T(4,128)}, bf16[1,3,2,3,384,512]{5,3,4,2,1,0:T(4,128)(2,1)S(1)}) fusion(f32[1,1,2,3,384,512]{5,3,4,2,1,0:T(4,128)} %get-tuple-element.86, f32[1,1,2,3,384,512]{5,3,4,2,1,0:T(4,128)} %get-tuple-element.87, f32[1,1,2,3,384,512]{5,3,4,2,1,0:T(4,128)} %get-tuple-element.85), kind=kLoop, calls=%fused_computation.10 | loop fusion | flops 10616832 | bytes 35389440 | tf_op jit(solution)/shard_map/add | solution.py:212
  264.8 4.8 collective-permute-start.5
  272.8 4.4 fusion.9
  277.2 63.5 %collective-permute-done.5 = bf16[1,2,3,384,512]{4,3,2,1,0:T(8,128)(2,1)} collective-permute-done((bf16[1,2,3,384,512]{4,3,2,1,0:T(8,128)(2,1)}, bf16[1,2,3,384,512]{4,3,2,1,0:T(8,128)(2,1)}, u32[]{:S(2)}, u32[]{:S(2)}) %collective-permute-start.5) | collective-permute-done | bytes 2359328 | tf_op jit(solution)/shard_map/ppermute | solution.py:17
  340.7 12.7 %collective-permute-done.4 = bf16[1,2,3,384,512]{4,3,2,1,0:T(8,128)(2,1)} collective-permute-done((bf16[1,2,3,384,512]{4,3,2,1,0:T(8,128)(2,1)}, bf16[1,2,3,384,512]{4,3,2,1,0:T(8,128)(2,1)}, u32[]{:S(2)}, u32[]{:S(2)}) %collective-permute-start.4) | collective-permute-done | bytes 2359328 | tf_op jit(solution)/shard_map/ppermute | solution.py:17
  353.5 10.7 %fusion.24 = (bf16[1,1,2,3,384,512]{5,3,4,2,1,0:T(4,128)(2,1)S(1)}, f32[1,1,2,3,384,512]{5,3,4,2,1,0:T(4,128)}) fusion(bf16[1,2,3,384,512]{4,3,2,1,0:T(8,128)(2,1)} %collective-permute-done.5, bf16[1,2,3,384,512]{4,3,2,1,0:T(8,128)(2,1)} %collective-permute-done.4, f32[1,3,2,3,384,512]{5,3,4,2,1,0:T(4,128)} %get-tuple-element.83), kind=kLoop, calls=%fused_computation.84 | loop fusion | flops 5898240 | bytes 16515072 | tf_op jit(solution)/shard_map/convert.6
  367.6 6.8 %collective-permute-start.7 = (bf16[1,1,2,384,512]{4,0,3,2,1:T(2,128)(2,1)}, bf16[1,1,2,384,512]{4,0,3,2,1:T(2,128)(2,1)}, u32[]{:S(2)}, u32[]{:S(2)}) collective-permute-start(bf16[1,1,2,384,512]{4,0,3,2,1:T(2,128)(2,1)} %get-tuple-element.115), channel_id=1, source_target_pairs={{0,1},{1,2},{2,3},{4,5},{5,6},{6,7},{8,9},{9,10},{10,11},{12,13},{... | collective-permute-start | bytes 2359304 | tf_op jit(solution)/shard_map/ppermute | solution.py:17
  375.7 7.2 %convolution_multiply_fusion = f32[4,128,384]{2,1,0:T(8,128)} fusion(bf16[3456,4,128]{0,2,1:T(8,128)(2,1)S(1)} %copy-done.3, bf16[4,384,3456]{1,2,0:T(8,128)(2,1)} %multiply_convert_fusion), kind=kOutput, calls=%fused_computation.45 | convolution fusion | flops 1359151104 | bytes 14942208 | tf_op jit(solution)/shard_map/while/body/eval_jaxpr/jhqk,jkhd->jqhd/dot_general | solution.py:34
  385.2 4.7 fusion.5
  389.9 7.0 %fusion.13 = f32[1,1,2,1,384,512]{5,3,4,2,1,0:T(1,128)S(1)} fusion(f32[1,1,2,3,384,512]{5,3,4,2,1,0:T(4,128)} %get-tuple-element.82, bf16[1,1,2,384,512]{4,0,3,2,1:T(2,128)(2,1)} %collective-permute-done.7, bf16[1,1,2,384,512]{4,0,3,2,1:T(2,128)(2,1)} %collective-permute-done.6), kind=kLoop, calls=%fused_computation.44 | loop fusion | flops 1572864 | bytes 4718592 | tf_op jit(solution)/shard_map/add | solution.py:225
  399.9 69.5 %all-reduce.23.cloned.1.call-done = f32[512,3072]{1,0:T(8,128)} async-done(((f32[512,3072]{1,0:T(8,128)}), f32[512,3072]{1,0:T(8,128)}) %all-reduce.23.cloned.1.call-update) | async-done | bytes 6291472 | tf_op jit(solution)/shard_map/psum | solution.py:236
  (98 shorter events, 69.7 us)
Async XLA Ops:
  7.2 50.0 %copy-start = (bf16[1,1,1,384,3072]{4,3,2,1,0:T(8,128)(2,1)S(1)}, bf16[1,1,1,384,3072]{4,3,2,1,0:T(8,128)(2,1)}, u32[]{:S(2)}) copy-start(bf16[1,1,1,384,3072]{4,3,2,1,0:T(8,128)(2,1)} %param.8) | copy-start | bytes 7077892
  7.2 50.0 %all-gather.2.cloned.1.call-start = ((), (), s32[]{:S(2)}) async-start(), calls=%async_computation | async-start | bytes 4718592 | tf_op jit(solution)/shard_map/all_gather | solution.py:154
  7.9 46.0 %copy-start.25 = (bf16[1,1,1,384,512]{4,3,2,1,0:T(8,128)(2,1)S(1)}, bf16[1,1,1,384,512]{4,3,2,1,0:T(8,128)(2,1)}, u32[]{:S(2)}) copy-start(bf16[1,1,1,384,512]{4,3,2,1,0:T(8,128)(2,1)} %param.5) | copy-start | bytes 1179652
  7.9 461.5 %all-reduce.23.cloned.1.call-start = ((), (), s32[]{:S(2)}) async-start(), calls=%async_computation.1 | async-start | bytes 12582912 | tf_op jit(solution)/shard_map/psum | solution.py:236
  9.2 22.5 %collective-permute-start.1 = (bf16[2,1,1,1,384,512]{5,4,3,2,1,0:T(8,128)(2,1)S(1)}, bf16[2,1,1,1,384,512]{5,4,3,2,1,0:T(8,128)(2,1)S(1)}, u32[]{:S(2)}, u32[]{:S(2)}) collective-permute-start(bf16[2,1,1,1,384,512]{5,4,3,2,1,0:T(8,128)(2,1)S(1)} %pad_maximum_fusion.4), channel_id=1, source_target_pairs={{4,0},{8,4},{12,8},{5,1},{9,5},{13,9},{6,2},{10,6},{14,10},{7,3},{... | collective-permute-start | bytes 2359304 | tf_op jit(solution)/shard_map/ppermute | solution.py:28
  10.5 22.4 %collective-permute-start = (bf16[2,1,1,1,384,512]{5,4,3,2,1,0:T(8,128)(2,1)S(1)}, bf16[2,1,1,1,384,512]{5,4,3,2,1,0:T(8,128)(2,1)S(1)}, u32[]{:S(2)}, u32[]{:S(2)}) collective-permute-start(bf16[2,1,1,1,384,512]{5,4,3,2,1,0:T(8,128)(2,1)S(1)} %pad_maximum_fusion.4), channel_id=1, source_target_pairs={{0,4},{4,8},{8,12},{1,5},{5,9},{9,13},{2,6},{6,10},{10,14},{3,7},{... | collective-permute-start | bytes 2359304 | tf_op jit(solution)/shard_map/ppermute | solution.py:27
  35.9 27.6 %collective-permute-start.3 = (bf16[2,1,3,1,384,512]{5,4,3,2,1,0:T(8,128)(2,1)}, bf16[2,1,3,1,384,512]{5,4,3,2,1,0:T(8,128)(2,1)}, u32[]{:S(2)}, u32[]{:S(2)}) collective-permute-start(bf16[2,1,3,1,384,512]{5,4,3,2,1,0:T(8,128)(2,1)} %pad_maximum_fusion.3), channel_id=1, source_target_pairs={{1,0},{2,1},{3,2},{5,4},{6,5},{7,6},{9,8},{10,9},{11,10},{13,12},{... | collective-permute-start | bytes 7077896 | tf_op jit(solution)/shard_map/ppermute | solution.py:28
  37.2 26.3 %collective-permute-start.2 = (bf16[2,1,3,1,384,512]{5,4,3,2,1,0:T(8,128)(2,1)}, bf16[2,1,3,1,384,512]{5,4,3,2,1,0:T(8,128)(2,1)}, u32[]{:S(2)}, u32[]{:S(2)}) collective-permute-start(bf16[2,1,3,1,384,512]{5,4,3,2,1,0:T(8,128)(2,1)} %pad_maximum_fusion.3), channel_id=1, source_target_pairs={{0,1},{1,2},{2,3},{4,5},{5,6},{6,7},{8,9},{9,10},{10,11},{12,13},{... | collective-permute-start | bytes 7077896 | tf_op jit(solution)/shard_map/ppermute | solution.py:27
  54.9 8.7 %copy-start.7 = (bf16[1,1,1,384,512]{4,3,2,1,0:T(8,128)(2,1)S(1)}, bf16[1,1,1,384,512]{4,3,2,1,0:T(8,128)(2,1)}, u32[]{:S(2)}) copy-start(bf16[1,1,1,384,512]{4,3,2,1,0:T(8,128)(2,1)} %param.7) | copy-start | bytes 1179652
  54.9 8.7 %copy-start.8 = (bf16[1,1,1,384,512]{4,3,2,1,0:T(8,128)(2,1)S(1)}, bf16[1,1,1,384,512]{4,3,2,1,0:T(8,128)(2,1)}, u32[]{:S(2)}) copy-start(bf16[1,1,1,384,512]{4,3,2,1,0:T(8,128)(2,1)} %param.6) | copy-start | bytes 1179652
  78.7 6.9 %copy-start.9 = (bf16[384,4,128]{2,1,0:T(4,128)(2,1)S(1)}, bf16[384,4,128]{2,1,0:T(4,128)(2,1)}, u32[]{:S(2)}) copy-start(bf16[384,4,128]{2,1,0:T(4,128)(2,1)} %reshape.243) | copy-start | bytes 1179652
  98.7 7.5 %copy-start.4 = (bf16[1,3,384,512]{3,2,1,0:T(8,128)(2,1)S(1)}, bf16[1,3,384,512]{3,2,1,0:T(8,128)(2,1)}, u32[]{:S(2)}) copy-start(bf16[1,3,384,512]{3,2,1,0:T(8,128)(2,1)} %get-tuple-element.108) | copy-start | bytes 3538948
  98.8 7.5 %copy-start.5 = (bf16[1,3,384,512]{3,2,1,0:T(8,128)(2,1)S(1)}, bf16[1,3,384,512]{3,2,1,0:T(8,128)(2,1)}, u32[]{:S(2)}) copy-start(bf16[1,3,384,512]{3,2,1,0:T(8,128)(2,1)} %get-tuple-element.112) | copy-start | bytes 3538948
  98.8 7.5 %copy-start.6 = (bf16[1,3,384,512]{3,2,1,0:T(8,128)(2,1)S(1)}, bf16[1,3,384,512]{3,2,1,0:T(8,128)(2,1)}, u32[]{:S(2)}) copy-start(bf16[1,3,384,512]{3,2,1,0:T(8,128)(2,1)} %get-tuple-element.113) | copy-start | bytes 3538948
  115.6 10.2 %copy-start.2 = (bf16[3456,4,128]{2,1,0:T(4,128)(2,1)S(1)}, bf16[3456,4,128]{2,1,0:T(4,128)(2,1)}, u32[]{:S(2)}) copy-start(bf16[3456,4,128]{2,1,0:T(4,128)(2,1)} %reshape.241) | copy-start | bytes 10616836
  115.6 10.2 %copy-start.10 = (f32[384,512]{0,1:T(8,128)S(1)}, f32[384,512]{0,1:T(8,128)}, u32[]{:S(2)}) copy-start(f32[384,512]{0,1:T(8,128)} %copy.100) | copy-start | bytes 2359300
  153.4 8.4 %copy-start.1 = (bf16[4,384,3456]{1,2,0:T(8,128)(2,1)S(1)}, bf16[4,384,3456]{1,2,0:T(8,128)(2,1)}, u32[]{:S(2)}) copy-start(bf16[4,384,3456]{1,2,0:T(8,128)(2,1)} %multiply_convert_fusion) | copy-start | bytes 31850500
  179.8 4.2 copy-start.21
  179.8 4.2 copy-start.22
  179.8 4.2 copy-start.23
  184.0 3.2 copy-start.20
  203.2 4.5 copy-start.16
  203.2 4.5 copy-start.17
  203.2 4.5 copy-start.18
  207.7 3.6 copy-start.13
  207.7 3.6 copy-start.14
  207.7 3.6 copy-start.15
  264.8 76.0 %collective-permute-start.5 = (bf16[1,2,3,384,512]{4,3,2,1,0:T(8,128)(2,1)}, bf16[1,2,3,384,512]{4,3,2,1,0:T(8,128)(2,1)}, u32[]{:S(2)}, u32[]{:S(2)}) collective-permute-start(bf16[1,2,3,384,512]{4,3,2,1,0:T(8,128)(2,1)} %copy.113), channel_id=1, source_target_pairs={{0,4},{4,8},{8,12},{1,5},{5,9},{9,13},{2,6},{6,10},{10,14},{3,7},{... | collective-permute-start | bytes 7077896 | tf_op jit(solution)/shard_map/ppermute | solution.py:17
  271.5 82.0 %collective-permute-start.4 = (bf16[1,2,3,384,512]{4,3,2,1,0:T(8,128)(2,1)}, bf16[1,2,3,384,512]{4,3,2,1,0:T(8,128)(2,1)}, u32[]{:S(2)}, u32[]{:S(2)}) collective-permute-start(bf16[1,2,3,384,512]{4,3,2,1,0:T(8,128)(2,1)} %copy.111), channel_id=1, source_target_pairs={{4,0},{8,4},{12,8},{5,1},{9,5},{13,9},{6,2},{10,6},{14,10},{7,3},{... | collective-permute-start | bytes 7077896 | tf_op jit(solution)/shard_map/ppermute | solution.py:17
  364.2 11.5 %copy-start.3 = (bf16[3456,4,128]{0,2,1:T(8,128)(2,1)S(1)}, bf16[3456,4,128]{0,2,1:T(8,128)(2,1)}, u32[]{:S(2)}) copy-start(bf16[3456,4,128]{0,2,1:T(8,128)(2,1)} %copy.102) | copy-start | bytes 10616836
  367.6 22.3 %collective-permute-start.7 = (bf16[1,1,2,384,512]{4,0,3,2,1:T(2,128)(2,1)}, bf16[1,1,2,384,512]{4,0,3,2,1:T(2,128)(2,1)}, u32[]{:S(2)}, u32[]{:S(2)}) collective-permute-start(bf16[1,1,2,384,512]{4,0,3,2,1:T(2,128)(2,1)} %get-tuple-element.115), channel_id=1, source_target_pairs={{0,1},{1,2},{2,3},{4,5},{5,6},{6,7},{8,9},{9,10},{10,11},{12,13},{... | collective-permute-start | bytes 2359304 | tf_op jit(solution)/shard_map/ppermute | solution.py:17
  374.4 15.5 %collective-permute-start.6 = (bf16[1,1,2,384,512]{4,0,3,2,1:T(2,128)(2,1)}, bf16[1,1,2,384,512]{4,0,3,2,1:T(2,128)(2,1)}, u32[]{:S(2)}, u32[]{:S(2)}) collective-permute-start(bf16[1,1,2,384,512]{4,0,3,2,1:T(2,128)(2,1)} %get-tuple-element.114), channel_id=1, source_target_pairs={{1,0},{2,1},{3,2},{5,4},{6,5},{7,6},{9,8},{10,9},{11,10},{13,12},{... | collective-permute-start | bytes 2359304 | tf_op jit(solution)/shard_map/ppermute | solution.py:17
  (4 other events, 8.2 us)
Sparse Core Ops, SparseCore 0:
  9.5 47.6 all-gather.1
  277.4 191.9 all-reduce.22
where the time goes:
time: 490 us; the launch traced here: 480 us
  waiting for transfers between devices  166 us (34%)
  other arithmetic  112 us (23%)
  local copies, waits for them, and re-layouts  91.6 us (19%)
  matrix products  58.7 us (12%)
  starting transfers between devices  26.9 us (5%)
  between operations  26 us (5%)
    ppermute x4, waiting for transfers between devices, shifted(): lax.ppermute(value, axis, [(source, source + steps) for source in range(f...  76.2 us
    psum x1, waiting for transfers between devices, on_device(): summed = lax.psum(local_term, ('dp', 'ha', 'wa'))  69.5 us
    dot_general x6, matrix products, product(): jnp.einsum(pattern, first_op, second_op, preferred_element_type=jnp.float32)  46.2 us
    another operation x5, local copies, waits for them, and re-layouts  23.5 us
    another operation x6, other arithmetic, spread_window(): return jnp.stack(spread_rows)  20.8 us
    another operation x2, other arithmetic, query_side(): return (query_grad, jnp.stack([key_part, value_part]))  19.3 us
    add x1, other arithmetic, on_device(): padded_grad = placed if padded_grad is None else padded_grad + placed  18.2 us
    ppermute x2, waiting for transfers between devices, with_halo(): after = lax.ppermute(first, axis, down)  15.6 us
  transfers between devices with their start and end apart: 10, of which 6 were waited for; matrix products, arithmetic and copies ran while one was open for 12% of the time, Pallas kernels for 0%

commit v1 on v0

--- a/solution.py
+++ b/solution.py
@@ -233,7 +233,9 @@
     local_term = lax.dot_general(
         flat_attn, flat_grad, (((0,), (0,)), ((), ())), preferred_element_type=jnp.float32
     )
-    summed = lax.psum(local_term, ("dp", "ha", "wa"))
+    summed = local_term
+    for over in (("ha", "wa"), "dp"):
+        summed = lax.psum(summed, over)
     weight_grad = lax.dynamic_slice_in_dim(summed, lax.axis_index("dp") * row_share, row_share, 0)
     return (outcome, query_grad, key_grad, value_grad, weight_grad)
 

time: 490 us -> 522 us (1.065)
  waiting for transfers between devices: 166 us -> 186 us
  local copies, waits for them, and re-layouts: 91.6 us -> 106 us
  starting transfers between devices: 26.9 us -> 20.5 us
    psum x1 -> x2, waiting for transfers between devices: 69.5 us -> 113 us  [on_device(): summed = lax.psum(summed, over)]
    ppermute x4, waiting for transfers between devices: 76.2 us -> 53.4 us  [shifted(): lax.ppermute(value, axis, [(source, source + steps) for source in range(f...]
    mul x1, local copies, waits for them, and re-layouts: 15.1 us -> 25.5 us  [query_back(): product('jhqk,jqhd->jkhd', score_grad, query_heads) * score_scale]
    ppermute x4, starting transfers between devices: 14.1 us -> 7.73 us  [shifted(): lax.ppermute(value, axis, [(source, source + steps) for source in range(f...]
  transfers between devices with their start and end apart: 10 -> 11, of which waited for: 6 -> 7; matrix products, arithmetic and copies ran while one was open for 12% -> 27% of each run, Pallas kernels for 0% -> 0%
where the time goes in v1:
time: 522 us; the launch traced here: 512 us
  waiting for transfers between devices  186 us (36%)
  other arithmetic  115 us (22%)
  local copies, waits for them, and re-layouts  106 us (20%)
  matrix products  58.6 us (11%)
  between operations  26 us (5%)
  starting transfers between devices  20.5 us (4%)
    psum x2, waiting for transfers between devices, on_device(): summed = lax.psum(summed, over)  113 us
    ppermute x4, waiting for transfers between devices, shifted(): lax.ppermute(value, axis, [(source, source + steps) for source in range(f...  53.4 us
    dot_general x6, matrix products, product(): jnp.einsum(pattern, first_op, second_op, preferred_element_type=jnp.float32)  46.2 us
    mul x1, local copies, waits for them, and re-layouts, query_back(): product('jhqk,jqhd->jkhd', score_grad, query_heads) * score_scale  25.5 us
    another operation x5, local copies, waits for them, and re-layouts  23.6 us
    another operation x2, other arithmetic, query_side(): return (query_grad, jnp.stack([key_part, value_part]))  20.5 us
    add x1, other arithmetic, on_device(): padded_grad = placed if padded_grad is None else padded_grad + placed  19.3 us
    another operation x6, other arithmetic, spread_window(): return jnp.stack(spread_rows)  19 us
  transfers between devices with their start and end apart: 11, of which 7 were waited for; matrix products, arithmetic and copies ran while one was open for 27% of the time, Pallas kernels for 0%

profile of v1, /device:TPU:0, one launch (start us, length us, event | category | flops | bytes accessed | tf_op | source)
XLA Modules:
  0.0 512.2 jit_solution(5778976981825777403)
XLA Ops:
  10.5 5.6 %collective-permute-start = (bf16[2,1,1,1,384,512]{5,4,3,2,1,0:T(8,128)(2,1)S(1)}, bf16[2,1,1,1,384,512]{5,4,3,2,1,0:T(8,128)(2,1)S(1)}, u32[]{:S(2)}, u32[]{:S(2)}) collective-permute-start(bf16[2,1,1,1,384,512]{5,4,3,2,1,0:T(8,128)(2,1)S(1)} %pad_maximum_fusion.4), channel_id=1, source_target_pairs={{0,4},{4,8},{8,12},{1,5},{5,9},{9,13},{2,6},{6,10},{10,14},{3,7},{... | collective-permute-start | bytes 2359304 | tf_op jit(solution)/shard_map/ppermute | solution.py:27
  16.1 15.6 %collective-permute-done.1 = bf16[2,1,1,1,384,512]{5,4,3,2,1,0:T(8,128)(2,1)S(1)} collective-permute-done((bf16[2,1,1,1,384,512]{5,4,3,2,1,0:T(8,128)(2,1)S(1)}, bf16[2,1,1,1,384,512]{5,4,3,2,1,0:T(8,128)(2,1)S(1)}, u32[]{:S(2)}, u32[]{:S(2)}) %collective-permute-start.1) | collective-permute-done | bytes 786464 | tf_op jit(solution)/shard_map/ppermute | solution.py:28
  37.2 4.5 collective-permute-start.2
  71.4 7.2 %reshape.242 = bf16[3456,4,128]{2,1,0:T(4,128)(2,1)} reshape(bf16[1,9,384,512]{3,2,1,0:T(8,128)(2,1)} %pad_maximum_fusion.2) | data formatting | bytes 7077888 | tf_op jit(solution)/shard_map/reshape.31
  78.7 6.8 %copy.102 = bf16[3456,4,128]{0,2,1:T(8,128)(2,1)} copy(bf16[3456,4,128]{2,1,0:T(4,128)(2,1)} %reshape.242) | data formatting | bytes 7077888 | tf_op jit(solution)/shard_map/reshape.31
  85.5 7.5 %bitcast_reduce_fusion = (f32[4,384]{1,0:T(4,128)S(1)}, f32[4,3456,384]{2,1,0:T(8,128)S(1)}) fusion(pred[3456]{0:T(1024)(128)(4,1)S(1)} %broadcast_in_dim.69, bf16[3456,4,128]{0,2,1:T(8,128)(2,1)} %copy.102, bf16[384,4,128]{2,1,0:T(4,128)(2,1)S(1)} %copy-done.10), kind=kOutput, calls=%fused_computation.2 | convolution fusion | flops 1374878208 | bytes 25175424 | tf_op jit(solution)/shard_map/while/body/eval_jaxpr/jqhd,jkhd->jhqk/dot_general | solution.py:34
  93.0 5.7 %fusion.1 = f32[4,384]{1,0:T(4,128)S(1)} fusion(f32[4,3456,384]{2,1,0:T(8,128)S(1)} %get-tuple-element.125, f32[4,384]{1,0:T(4,128)S(1)} %get-tuple-element.124, pred[3456]{0:T(1024)(128)(4,1)S(1)} %broadcast_in_dim.69), kind=kLoop, calls=%fused_computation.4 | loop fusion | flops 21232128 | bytes 21249408 | tf_op jit(solution)/shard_map/while/body/eval_jaxpr/reduce_sum | solution.py:92
  98.7 7.4 %fusion.3 = bf16[4,384,3456]{1,2,0:T(8,128)(2,1)} fusion(f32[4,3456,384]{2,1,0:T(8,128)S(1)} %get-tuple-element.125, f32[4,384]{1,0:T(4,128)S(1)} %log_add_fusion, pred[3456]{0:T(1024)(128)(4,1)S(1)} %broadcast_in_dim.69), kind=kLoop, calls=%fused_computation.6 | loop fusion | flops 21233664 | bytes 31860096 | tf_op jit(solution)/shard_map/while/body/eval_jaxpr/convert_element_type | solution.py:93
  108.0 7.5 %reshape.241 = bf16[3456,4,128]{2,1,0:T(4,128)(2,1)} reshape(bf16[1,9,384,512]{3,2,1,0:T(8,128)(2,1)} %pad_maximum_fusion.1) | data formatting | bytes 7077888 | tf_op jit(solution)/shard_map/reshape.41
  115.5 10.3 %convolution_bitcast_fusion = f32[1,3456,4,128]{1,3,2,0:T(8,128)} fusion(bf16[384,4,128]{0,2,1:T(8,128)(2,1)S(1)} %bitcast.185, bf16[4,384,3456]{1,2,0:T(8,128)(2,1)} %fusion.3), kind=kOutput, calls=%fused_computation.15 | convolution fusion | flops 1358954496 | bytes 18087936 | tf_op jit(solution)/shard_map/while/body/eval_jaxpr/jhqk,jqhd->jkhd/dot_general | solution.py:34
  125.8 6.3 %multiply_reduce_fusion = (f32[384,4]{0,1:T(4,128)S(1)}, bf16[4,128,384]{2,1,0:T(8,128)(2,1)S(1)}) fusion(f32[1,384,4,128]{1,3,2,0:T(8,128)S(1)} %bitcast.195, bf16[4,384,3456]{1,2,0:T(8,128)(2,1)} %fusion.3, bf16[3456,4,128]{2,1,0:T(4,128)(2,1)S(1)} %copy-done.3), kind=kOutput, calls=%fused_computation.75 | convolution fusion | flops 1359739392 | bytes 15341568 | tf_op jit(solution)/shard_map/while/body/eval_jaxpr/jhqk,jkhd->jqhd/dot_general | solution.py:34
  132.1 12.1 %multiply_convert_fusion = bf16[4,384,3456]{1,2,0:T(8,128)(2,1)} fusion(bf16[4,384,3456]{1,2,0:T(8,128)(2,1)} %fusion.3, bf16[384,4,128]{0,2,1:T(8,128)(2,1)S(1)} %bitcast.186, f32[4,384]{1,0:T(4,128)S(1)} %bitcast.197, bf16[3456,4,128]{2,1,0:T(4,128)(2,1)} %reshape.241), kind=kOutput, calls=%fused_computation.7 | convolution fusion | flops 1380188160 | bytes 25171968 | tf_op jit(solution)/shard_map/while/body/eval_jaxpr/jqhd,jkhd->jhqk/dot_general | solution.py:34
  144.2 9.1 %copy.108 = f32[1,3456,4,128]{3,2,0,1:T(4,128)} copy(f32[1,3456,4,128]{1,3,2,0:T(8,128)} %convolution_bitcast_fusion) | data formatting | bytes 14155776 | tf_op jit(solution)/shard_map/while/body/eval_jaxpr/jhqk,jqhd->jkhd/transpose | solution.py:34
  153.3 8.3 %slice_bitcast_fusion.23 = (f32[1,384,512]{2,0,1:T(1,128)}, f32[1,384,512]{2,0,1:T(1,128)}, f32[1,384,512]{2,0,1:T(1,128)}, f32[1,384,512]{2,0,1:T(1,128)}, f32[...) fusion(f32[1,3,3,384,512]{4,0,3,2,1:T(1,128)} %bitcast.183), kind=kLoop, calls=%fused_computation.64 | loop fusion | bytes 14155776 | tf_op jit(solution)/shard_map/while/body/eval_jaxpr/squeeze | solution.py:64
  164.6 25.5 %copy.105 = f32[1,3456,4,128]{3,2,0,1:T(4,128)S(1)} copy(f32[1,3456,4,128]{3,1,2,0:T(8,128)S(1)} %multiply_bitcast_fusion) | data formatting | bytes 14155776 | tf_op jit(solution)/shard_map/while/body/eval_jaxpr/mul | solution.py:120
  190.2 4.2 slice_bitcast_fusion.32
  194.3 4.4 fusion.9
  210.0 10.6 %maximum_bitcast_fusion.2 = f32[1,3,3,384,512]{4,2,3,1,0:T(4,128)} fusion(f32[1,3,384,512]{3,1,2,0:T(4,128)} %add_bitcast_fusion, f32[1,3,384,512]{3,1,2,0:T(4,128)} %add_bitcast_fusion.1, f32[1,3,384,512]{3,1,2,0:T(4,128)} %add_bitcast_fusion.2), kind=kLoop, calls=%fused_computation.12 | loop fusion | flops 3538944 | bytes 14155776 | tf_op jit(solution)/shard_map/while/body/eval_jaxpr/stack | solution.py:198
  230.2 9.8 %maximum_bitcast_fusion.1 = f32[1,3,3,384,512]{4,2,3,1,0:T(4,128)} fusion(f32[1,3,384,512]{3,1,2,0:T(4,128)} %add_bitcast_fusion.3, f32[1,3,384,512]{3,1,2,0:T(4,128)} %add_bitcast_fusion.4, f32[1,3,384,512]{3,1,2,0:T(4,128)} %add_bitcast_fusion.5), kind=kLoop, calls=%fused_computation.11 | loop fusion | flops 3538944 | bytes 14155776 | tf_op jit(solution)/shard_map/while/body/eval_jaxpr/stack | solution.py:198
  240.0 10.6 %maximum_bitcast_fusion = f32[1,1,2,3,3,384,512]{6,4,5,3,2,1,0:T(4,128)S(1)} fusion(f32[1,3,3,384,512]{4,2,3,1,0:T(4,128)} %maximum_bitcast_fusion.2, f32[1,3,3,384,512]{4,2,3,1,0:T(4,128)} %maximum_bitcast_fusion.1), kind=kLoop, calls=%fused_computation.9 | loop fusion | flops 3538944 | bytes 28311552 | tf_op jit(solution)/shard_map/reshape | solution.py:203
  250.6 7.9 %slice_bitcast_fusion.2 = (f32[1,1,2,3,384,512]{5,3,4,2,1,0:T(4,128)}, f32[1,1,2,3,384,512]{5,3,4,2,1,0:T(4,128)}, f32[1,1,2,3,384,512]{5,3,4,2,1,0:T(4,128)}) fusion(f32[1,1,2,3,3,384,512]{6,4,5,3,2,1,0:T(4,128)S(1)} %maximum_bitcast_fusion), kind=kLoop, calls=%fused_computation.20 | loop fusion | bytes 28311552 | tf_op jit(solution)/shard_map/squeeze | solution.py:209
  258.5 19.3 %pad_add_fusion = (f32[1,3,2,3,384,512]{5,3,4,2,1,0:T(4,128)}, bf16[1,3,2,3,384,512]{5,3,4,2,1,0:T(4,128)(2,1)}) fusion(f32[1,1,2,3,384,512]{5,3,4,2,1,0:T(4,128)} %get-tuple-element.86, f32[1,1,2,3,384,512]{5,3,4,2,1,0:T(4,128)} %get-tuple-element.87, f32[1,1,2,3,384,512]{5,3,4,2,1,0:T(4,128)} %get-tuple-element.85), kind=kLoop, calls=%fused_computation.10 | loop fusion | flops 10616832 | bytes 35389440 | tf_op jit(solution)/shard_map/add | solution.py:212
  277.9 67.7 %all-reduce.24.cloned.1.call-done = f32[512,3072]{1,0:T(8,128)} async-done(((f32[512,3072]{1,0:T(8,128)}), f32[512,3072]{1,0:T(8,128)}) %all-reduce.24.cloned.1.call-update) | async-done | bytes 6291472 | tf_op jit(solution)/shard_map/psum | solution.py:238
  345.6 4.6 slice_bitcast_fusion.4
  358.9 47.1 %collective-permute-done.5 = bf16[1,2,3,384,512]{4,3,2,1,0:T(8,128)(2,1)S(1)} collective-permute-done((bf16[1,2,3,384,512]{4,3,2,1,0:T(8,128)(2,1)}, bf16[1,2,3,384,512]{4,3,2,1,0:T(8,128)(2,1)S(1)}, u32[]{:S(2)}, u32[]{:S(2)}) %collective-permute-start.5) | collective-permute-done | bytes 2359328 | tf_op jit(solution)/shard_map/ppermute | solution.py:17
  406.1 6.2 %collective-permute-done.4 = bf16[1,2,3,384,512]{4,3,2,1,0:T(8,128)(2,1)} collective-permute-done((bf16[1,2,3,384,512]{4,3,2,1,0:T(8,128)(2,1)}, bf16[1,2,3,384,512]{4,3,2,1,0:T(8,128)(2,1)}, u32[]{:S(2)}, u32[]{:S(2)}) %collective-permute-start.4) | collective-permute-done | bytes 2359328 | tf_op jit(solution)/shard_map/ppermute | solution.py:17
  412.3 13.0 %fusion.24 = (bf16[1,1,2,3,384,512]{5,3,4,2,1,0:T(4,128)(2,1)S(1)}, f32[1,1,2,3,384,512]{5,3,4,2,1,0:T(4,128)}) fusion(bf16[1,2,3,384,512]{4,3,2,1,0:T(8,128)(2,1)S(1)} %collective-permute-done.5, bf16[1,2,3,384,512]{4,3,2,1,0:T(8,128)(2,1)} %collective-permute-done.4, f32[1,3,2,3,384,512]{5,3,4,2,1,0:T(4,128)} %get-tuple-element.83), kind=kLoop, calls=%fused_computation.84 | loop fusion | flops 5898240 | bytes 16515072 | tf_op jit(solution)/shard_map/convert.6
  431.6 7.1 %convolution_multiply_fusion = f32[4,128,384]{2,1,0:T(8,128)S(1)} fusion(bf16[3456,4,128]{0,2,1:T(8,128)(2,1)S(1)} %copy-done.4, bf16[4,384,3456]{1,2,0:T(8,128)(2,1)} %multiply_convert_fusion), kind=kOutput, calls=%fused_computation.45 | convolution fusion | flops 1359151104 | bytes 14942208 | tf_op jit(solution)/shard_map/while/body/eval_jaxpr/jhqk,jkhd->jqhd/dot_general | solution.py:34
  439.8 4.7 fusion.5
  445.7 7.1 %fusion.13 = f32[1,1,2,1,384,512]{5,3,4,2,1,0:T(1,128)S(1)} fusion(f32[1,1,2,3,384,512]{5,3,4,2,1,0:T(4,128)} %get-tuple-element.82, bf16[1,1,2,384,512]{4,0,3,2,1:T(2,128)(2,1)} %copy-done.33, bf16[1,1,2,384,512]{4,0,3,2,1:T(2,128)(2,1)} %collective-permute-done.6), kind=kLoop, calls=%fused_computation.44 | loop fusion | flops 1572864 | bytes 4718592 | tf_op jit(solution)/shard_map/add | solution.py:225
  455.7 45.6 %all-reduce.26.cloned.1.call-done = f32[512,3072]{1,0:T(8,128)} async-done(((f32[512,3072]{1,0:T(8,128)}), f32[512,3072]{1,0:T(8,128)}) %all-reduce.26.cloned.1.call-update) | async-done | bytes 6291472 | tf_op jit(solution)/shard_map/psum | solution.py:238
  501.3 3.9 constant_dynamic-slice_fusion
  (119 shorter events, 73.0 us)
Async XLA Ops:
  7.2 50.0 %copy-start = (bf16[1,1,1,384,3072]{4,3,2,1,0:T(8,128)(2,1)S(1)}, bf16[1,1,1,384,3072]{4,3,2,1,0:T(8,128)(2,1)}, u32[]{:S(2)}) copy-start(bf16[1,1,1,384,3072]{4,3,2,1,0:T(8,128)(2,1)} %param.8) | copy-start | bytes 7077892
  7.2 50.0 %all-gather.2.cloned.1.call-start = ((), (), s32[]{:S(2)}) async-start(), calls=%async_computation | async-start | bytes 4718592 | tf_op jit(solution)/shard_map/all_gather | solution.py:154
  7.9 46.1 %copy-start.34 = (bf16[1,1,1,384,512]{4,3,2,1,0:T(8,128)(2,1)S(1)}, bf16[1,1,1,384,512]{4,3,2,1,0:T(8,128)(2,1)}, u32[]{:S(2)}) copy-start(bf16[1,1,1,384,512]{4,3,2,1,0:T(8,128)(2,1)} %param.5) | copy-start | bytes 1179652
  7.9 337.6 %all-reduce.24.cloned.1.call-start = ((), (), s32[]{:S(2)}) async-start(), calls=%async_computation.1 | async-start | bytes 12582912 | tf_op jit(solution)/shard_map/psum | solution.py:238
  9.2 22.5 %collective-permute-start.1 = (bf16[2,1,1,1,384,512]{5,4,3,2,1,0:T(8,128)(2,1)S(1)}, bf16[2,1,1,1,384,512]{5,4,3,2,1,0:T(8,128)(2,1)S(1)}, u32[]{:S(2)}, u32[]{:S(2)}) collective-permute-start(bf16[2,1,1,1,384,512]{5,4,3,2,1,0:T(8,128)(2,1)S(1)} %pad_maximum_fusion.4), channel_id=1, source_target_pairs={{4,0},{8,4},{12,8},{5,1},{9,5},{13,9},{6,2},{10,6},{14,10},{7,3},{... | collective-permute-start | bytes 2359304 | tf_op jit(solution)/shard_map/ppermute | solution.py:28
  10.5 22.4 %collective-permute-start = (bf16[2,1,1,1,384,512]{5,4,3,2,1,0:T(8,128)(2,1)S(1)}, bf16[2,1,1,1,384,512]{5,4,3,2,1,0:T(8,128)(2,1)S(1)}, u32[]{:S(2)}, u32[]{:S(2)}) collective-permute-start(bf16[2,1,1,1,384,512]{5,4,3,2,1,0:T(8,128)(2,1)S(1)} %pad_maximum_fusion.4), channel_id=1, source_target_pairs={{0,4},{4,8},{8,12},{1,5},{5,9},{9,13},{2,6},{6,10},{10,14},{3,7},{... | collective-permute-start | bytes 2359304 | tf_op jit(solution)/shard_map/ppermute | solution.py:27
  36.0 27.6 %collective-permute-start.3 = (bf16[2,1,3,1,384,512]{5,4,3,2,1,0:T(8,128)(2,1)}, bf16[2,1,3,1,384,512]{5,4,3,2,1,0:T(8,128)(2,1)}, u32[]{:S(2)}, u32[]{:S(2)}) collective-permute-start(bf16[2,1,3,1,384,512]{5,4,3,2,1,0:T(8,128)(2,1)} %pad_maximum_fusion.3), channel_id=1, source_target_pairs={{1,0},{2,1},{3,2},{5,4},{6,5},{7,6},{9,8},{10,9},{11,10},{13,12},{... | collective-permute-start | bytes 7077896 | tf_op jit(solution)/shard_map/ppermute | solution.py:28
  37.2 26.3 %collective-permute-start.2 = (bf16[2,1,3,1,384,512]{5,4,3,2,1,0:T(8,128)(2,1)}, bf16[2,1,3,1,384,512]{5,4,3,2,1,0:T(8,128)(2,1)}, u32[]{:S(2)}, u32[]{:S(2)}) collective-permute-start(bf16[2,1,3,1,384,512]{5,4,3,2,1,0:T(8,128)(2,1)} %pad_maximum_fusion.3), channel_id=1, source_target_pairs={{0,1},{1,2},{2,3},{4,5},{5,6},{6,7},{8,9},{9,10},{10,11},{12,13},{... | collective-permute-start | bytes 7077896 | tf_op jit(solution)/shard_map/ppermute | solution.py:27
  54.9 8.7 %copy-start.8 = (bf16[1,1,1,384,512]{4,3,2,1,0:T(8,128)(2,1)S(1)}, bf16[1,1,1,384,512]{4,3,2,1,0:T(8,128)(2,1)}, u32[]{:S(2)}) copy-start(bf16[1,1,1,384,512]{4,3,2,1,0:T(8,128)(2,1)} %param.7) | copy-start | bytes 1179652
  54.9 8.7 %copy-start.9 = (bf16[1,1,1,384,512]{4,3,2,1,0:T(8,128)(2,1)S(1)}, bf16[1,1,1,384,512]{4,3,2,1,0:T(8,128)(2,1)}, u32[]{:S(2)}) copy-start(bf16[1,1,1,384,512]{4,3,2,1,0:T(8,128)(2,1)} %param.6) | copy-start | bytes 1179652
  78.7 6.8 %copy-start.10 = (bf16[384,4,128]{2,1,0:T(4,128)(2,1)S(1)}, bf16[384,4,128]{2,1,0:T(4,128)(2,1)}, u32[]{:S(2)}) copy-start(bf16[384,4,128]{2,1,0:T(4,128)(2,1)} %reshape.243) | copy-start | bytes 1179652
  98.7 7.4 %copy-start.5 = (bf16[1,3,384,512]{3,2,1,0:T(8,128)(2,1)S(1)}, bf16[1,3,384,512]{3,2,1,0:T(8,128)(2,1)}, u32[]{:S(2)}) copy-start(bf16[1,3,384,512]{3,2,1,0:T(8,128)(2,1)} %get-tuple-element.108) | copy-start | bytes 3538948
  98.7 7.4 %copy-start.6 = (bf16[1,3,384,512]{3,2,1,0:T(8,128)(2,1)S(1)}, bf16[1,3,384,512]{3,2,1,0:T(8,128)(2,1)}, u32[]{:S(2)}) copy-start(bf16[1,3,384,512]{3,2,1,0:T(8,128)(2,1)} %get-tuple-element.112) | copy-start | bytes 3538948
  98.7 7.4 %copy-start.7 = (bf16[1,3,384,512]{3,2,1,0:T(8,128)(2,1)S(1)}, bf16[1,3,384,512]{3,2,1,0:T(8,128)(2,1)}, u32[]{:S(2)}) copy-start(bf16[1,3,384,512]{3,2,1,0:T(8,128)(2,1)} %get-tuple-element.113) | copy-start | bytes 3538948
  115.5 10.3 %copy-start.3 = (bf16[3456,4,128]{2,1,0:T(4,128)(2,1)S(1)}, bf16[3456,4,128]{2,1,0:T(4,128)(2,1)}, u32[]{:S(2)}) copy-start(bf16[3456,4,128]{2,1,0:T(4,128)(2,1)} %reshape.241) | copy-start | bytes 10616836
  115.5 10.3 %copy-start.11 = (f32[384,512]{0,1:T(8,128)S(1)}, f32[384,512]{0,1:T(8,128)}, u32[]{:S(2)}) copy-start(f32[384,512]{0,1:T(8,128)} %copy.100) | copy-start | bytes 2359300
  153.3 8.3 %copy-start.2 = (bf16[4,384,3456]{1,2,0:T(8,128)(2,1)S(1)}, bf16[4,384,3456]{1,2,0:T(8,128)(2,1)}, u32[]{:S(2)}) copy-start(bf16[4,384,3456]{1,2,0:T(8,128)(2,1)} %multiply_convert_fusion) | copy-start | bytes 31850500
  198.8 302.5 %all-reduce.26.cloned.1.call-start = ((), (), s32[]{:S(2)}) async-start(), calls=%async_computation.2 | async-start | bytes 12582912 | tf_op jit(solution)/shard_map/psum | solution.py:238
  198.9 4.7 copy-start.26
  198.9 4.7 copy-start.27
  198.9 4.7 copy-start.28
  203.5 3.3 copy-start.21
  203.5 3.3 copy-start.22
  210.0 10.6 %copy-start.23 = (f32[1,384,512]{2,0,1:T(1,128)S(1)}, f32[1,384,512]{2,0,1:T(1,128)}, u32[]{:S(2)}) copy-start(f32[1,384,512]{2,0,1:T(1,128)} %get-tuple-element.91) | copy-start | bytes 2359300
  210.0 10.6 %copy-start.24 = (f32[1,384,512]{2,0,1:T(1,128)S(1)}, f32[1,384,512]{2,0,1:T(1,128)}, u32[]{:S(2)}) copy-start(f32[1,384,512]{2,0,1:T(1,128)} %get-tuple-element.92) | copy-start | bytes 2359300
  210.0 10.6 %copy-start.25 = (f32[1,384,512]{2,0,1:T(1,128)S(1)}, f32[1,384,512]{2,0,1:T(1,128)}, u32[]{:S(2)}) copy-start(f32[1,384,512]{2,0,1:T(1,128)} %get-tuple-element.93) | copy-start | bytes 2359300
  352.1 54.0 %collective-permute-start.5 = (bf16[1,2,3,384,512]{4,3,2,1,0:T(8,128)(2,1)}, bf16[1,2,3,384,512]{4,3,2,1,0:T(8,128)(2,1)S(1)}, u32[]{:S(2)}, u32[]{:S(2)}) collective-permute-start(bf16[1,2,3,384,512]{4,3,2,1,0:T(8,128)(2,1)} %copy.113), channel_id=1, source_target_pairs={{0,4},{4,8},{8,12},{1,5},{5,9},{9,13},{2,6},{6,10},{10,14},{3,7},{... | collective-permute-start | bytes 7077896 | tf_op jit(solution)/shard_map/ppermute | solution.py:17
  357.6 54.7 %collective-permute-start.4 = (bf16[1,2,3,384,512]{4,3,2,1,0:T(8,128)(2,1)}, bf16[1,2,3,384,512]{4,3,2,1,0:T(8,128)(2,1)}, u32[]{:S(2)}, u32[]{:S(2)}) collective-permute-start(bf16[1,2,3,384,512]{4,3,2,1,0:T(8,128)(2,1)} %copy.111), channel_id=1, source_target_pairs={{4,0},{8,4},{12,8},{5,1},{9,5},{13,9},{6,2},{10,6},{14,10},{7,3},{... | collective-permute-start | bytes 7077896 | tf_op jit(solution)/shard_map/ppermute | solution.py:17
  425.3 6.3 %copy-start.4 = (bf16[3456,4,128]{0,2,1:T(8,128)(2,1)S(1)}, bf16[3456,4,128]{0,2,1:T(8,128)(2,1)}, u32[]{:S(2)}) copy-start(bf16[3456,4,128]{0,2,1:T(8,128)(2,1)} %copy.102) | copy-start | bytes 10616836
  428.7 15.9 %collective-permute-start.7 = (bf16[1,1,2,384,512]{4,0,3,2,1:T(2,128)(2,1)}, bf16[1,1,2,384,512]{4,0,3,2,1:T(2,128)(2,1)S(1)}, u32[]{:S(2)}, u32[]{:S(2)}) collective-permute-start(bf16[1,1,2,384,512]{4,0,3,2,1:T(2,128)(2,1)} %get-tuple-element.115), channel_id=1, source_target_pairs={{0,1},{1,2},{2,3},{4,5},{5,6},{6,7},{8,9},{9,10},{10,11},{12,13},{... | collective-permute-start | bytes 2359304 | tf_op jit(solution)/shard_map/ppermute | solution.py:17
  430.1 14.5 %collective-permute-start.6 = (bf16[1,1,2,384,512]{4,0,3,2,1:T(2,128)(2,1)}, bf16[1,1,2,384,512]{4,0,3,2,1:T(2,128)(2,1)}, u32[]{:S(2)}, u32[]{:S(2)}) collective-permute-start(bf16[1,1,2,384,512]{4,0,3,2,1:T(2,128)(2,1)} %get-tuple-element.114), channel_id=1, source_target_pairs={{1,0},{2,1},{3,2},{5,4},{6,5},{7,6},{9,8},{10,9},{11,10},{13,12},{... | collective-permute-start | bytes 2359304 | tf_op jit(solution)/shard_map/ppermute | solution.py:17
  454.8 50.4 %copy-start.1 = (bf16[1,1,1,384,3072]{4,3,2,1,0:T(8,128)(2,1)S(1)}, bf16[1,1,1,384,3072]{4,3,2,1,0:T(8,128)(2,1)}, u32[]{:S(2)}) copy-start(bf16[1,1,1,384,3072]{4,3,2,1,0:T(8,128)(2,1)} %param.8) | copy-start | bytes 7077892
  (14 other events, 32.8 us)
Sparse Core Ops, SparseCore 0:
  9.5 47.6 all-gather.1
  198.9 146.5 all-reduce.23
  348.0 153.2 all-reduce.25
